TPU v7x, 512 devices: a whole 4x8x8 slice. The times are simulated.
512 devices in a mesh: row: 8 (over z), col: 16 (over y, core), vox: 4 (over x).
Axes of the slice: x: 4, y: 8, z: 8, core: 2. Of those that a mesh axis runs over, the one named last changes fastest.
Arguments:
- panel_top: bfloat16 [1024, 1024], P('row', ('col', 'vox')), may hold values from -0.059814453 to 0.059814453
- panel_low: bfloat16 [8192, 1024], P('row', ('col', 'vox')), may hold values from -1.1953125 to 1.1953125
- panel_next: bfloat16 [8192, 1024], P('row', ('col', 'vox')), may hold values from -1.1953125 to 1.1953125
- gram_rest: bfloat16 [8192, 8192], P('row', ('col', 'vox')), may hold values from -18 to 18
- inverses: bfloat16 [2, 1024, 1024], P(None, 'row'), as said below
- right_top: bfloat16 [2, 1024, 8192], P(None, None, ('col', 'vox')), may hold values from -1.796875 to 1.796875
- right_low: bfloat16 [8192, 8192], P('row', ('col', 'vox')), may hold values from -24 to 24
Outputs:
- factor: bfloat16 [2, 8192, 1024], P(None, 'row', ('col', 'vox'))
- solved: bfloat16 [2, 1024, 8192], P(None, None, ('col', 'vox'))
- trailing: float32 [8192, 8192], P('row', ('col', 'vox'))
- residual: float32 [8192, 8192], P('row', ('col', 'vox'))
Inputs may be any that keep to these rules, and one draw needn't show every extreme that they name: Each inverses[k] is lower triangular with diagonal entries from 1 to 2.
All inputs are finite; a program needn't handle non-finite values.
Results may differ from a plain program's by a relative error of at most 0.0057.
Values may be sent and summed in bfloat16 or wider, within the bound.
No kernel may reach another device: no remote copies, remote signals or barrier semaphores. Data moves between devices by JAX's collectives and lax.ppermute only.
A program may use at most 64 MiB of HBM per device.

v0:
```python
import jax
import jax.numpy as jnp
import numpy as np
from jax import lax
from jax.sharding import Mesh
from jax.sharding import PartitionSpec as P


def contract(left, right, dims):
    return lax.dot_general(left, right, (dims, ((), ())), preferred_element_type=jnp.float32)


def gather_small(block, axis, size):
    out = lax.all_to_all(jnp.tile(block, (size, 1)), axis, 0, 0, tiled=True)
    return out.reshape((size,) + block.shape)


def per_device(sizes, panel_top, panel_low, panel_next, gram_rest, inverses, right_top, right_low):
    rows, ys, cores, voxes = sizes
    axes = ("row", "y", "core", "vox")
    order = np.arange(rows * ys * cores * voxes).reshape(sizes)
    swap = list(zip(order.ravel().tolist(), order.transpose(1, 0, 2, 3).ravel().tolist()))
    y = lax.axis_index("y")
    core = lax.axis_index("core")
    vox = lax.axis_index("vox")
    width = panel_low.shape[1]
    rest_cols = gram_rest.shape[1]
    bf16 = jnp.bfloat16
    whole = lax.all_gather(inverses, "row", axis=1, tiled=True)
    top = gather_small(panel_top.T, "row", rows).transpose(1, 0, 2).reshape(width, -1)
    panels = jnp.stack([top, panel_low.T, panel_next.T])
    panels = lax.all_gather(panels, ("y", "core", "vox"), axis=1, tiled=True)
    low = panels[0:2].transpose(1, 0, 2).reshape(panels.shape[1], -1)
    first = contract(whole[0], low, ((1,), (0,))).astype(bf16)
    first_top, first_low = (first[:, : panels.shape[2]], first[:, panels.shape[2] :])
    updated = (panels[2].astype(jnp.float32) - contract(first_top, first_low, ((0,), (0,)))).astype(
        bf16
    )
    second_low = contract(whole[1], updated, ((1,), (0,))).astype(bf16)
    start = (core * voxes + vox) * rest_cols
    first_rows = lax.ppermute(lax.dynamic_slice_in_dim(first_low, start, rest_cols, 1), axes, swap)
    second_rows = lax.ppermute(
        lax.dynamic_slice_in_dim(second_low, start, rest_cols, 1), axes, swap
    )
    first_solve = contract(whole[0], right_top[0], ((1,), (0,))).astype(bf16)
    top_new = (
        right_top[1].astype(jnp.float32) - contract(first_top, first_solve, ((0,), (0,)))
    ).astype(bf16)
    second_solve = contract(whole[1], top_new, ((1,), (0,))).astype(bf16)
    residual = (
        right_low.astype(jnp.float32)
        - contract(first_low, first_solve, ((0,), (0,)))
        - contract(second_low, second_solve, ((0,), (0,)))
    )
    trailing = (
        gram_rest.astype(jnp.float32)
        - contract(first_low, first_rows, ((0,), (0,)))
        - contract(second_low, second_rows, ((0,), (0,)))
    )
    own = ((y * cores + core) * voxes + vox) * width
    factor = jnp.stack(
        [
            lax.dynamic_slice_in_dim(first_low, own, width, 0).T,
            lax.dynamic_slice_in_dim(second_low, own, width, 0).T,
        ]
    )
    solved = jnp.stack([first_solve, second_solve])
    return (factor, solved, trailing, residual)


def solution(mesh):
    cores = 2
    sizes = (mesh.shape["row"], mesh.shape["col"] // cores, cores, mesh.shape["vox"])
    split = Mesh(mesh.devices.reshape(sizes), ("row", "y", "core", "vox"))
    cols = ("y", "core", "vox")
    in_specs = (
        P("row", cols),
        P("row", cols),
        P("row", cols),
        P("row", cols),
        P(None, "row", None),
        P(None, None, cols),
        P("row", cols),
    )
    out_specs = (P(None, "row", cols), P(None, None, cols), P("row", cols), P("row", cols))

    def body(*args):
        return per_device(sizes, *args)

    return jax.shard_map(body, mesh=split, in_specs=in_specs, out_specs=out_specs, check_vma=False)
```

profile of v0, /device:TPU:16, one launch (start us, length us, event | category | flops | bytes accessed | tf_op | source)
XLA Modules:
  0.0 259.9 jit_solution(18153763955404550325)
XLA Ops:
  7.2 0.0 all-gather.5.cloned.1.call-start
  7.2 0.7 all-gather.5.cloned.1.call-update
  7.9 0.0 all-gather.3.cloned.1.call-start
  7.9 0.7 tile.2
  8.6 18.1 %all_to_all.6 = bf16[8,16,128]{2,1,0:T(8,128)(2,1)S(1)} all-to-all(bf16[8,16,128]{2,1,0:T(8,128)(2,1)S(1)} %tile.2), channel_id=1, replica_groups=mesh['row'=8,'y'=8,'core'=2,'vox'=4] {'row'}, dimensions={0} | all-to-all | bytes 65536 | tf_op jit(solution)/shard_map/all_to_all | solution.py:14
  26.8 1.4 pad_maximum_fusion.1
  28.2 0.0 all-gather.3.cloned.1.call-update
  28.3 44.6 %all-gather.5.cloned.1.call-done = bf16[2,1024,1024]{2,1,0:T(8,128)(2,1)} async-done(((bf16[2,128,1024]{2,1,0:T(8,128)(2,1)}), bf16[2,1024,1024]{2,1,0:T(8,128)(2,1)}) %all-gather.5.cloned.1.call-update) | async-done | bytes 4194320 | tf_op jit(solution)/shard_map/all_gather | solution.py:29
  72.9 2.3 fusion.17
  75.2 0.0 copy-start.2
  75.2 85.2 %all-gather.3.cloned.1.call-done = bf16[3,1024,1024]{2,1,0:T(8,128)(2,1)} async-done(((bf16[3,16,1024]{2,1,0:T(8,128)(2,1)}), bf16[3,1024,1024]{2,1,0:T(8,128)(2,1)}) %all-gather.3.cloned.1.call-update) | async-done | bytes 6291472 | tf_op jit(solution)/shard_map/all_gather | solution.py:32
  160.4 4.7 %slice.34 = bf16[2,1024,1024]{2,1,0:T(8,128)(2,1)} slice(bf16[3,1024,1024]{2,1,0:T(8,128)(2,1)} %all-gather.3.cloned.1.call-done), slice={[0:2], [0:1024], [0:1024]} | slice | bytes 8388608 | tf_op jit(solution)/shard_map/slice | solution.py:33
  165.1 6.2 %copy.22 = bf16[2,1024,1024]{1,2,0:T(8,128)(2,1)} copy(bf16[2,1024,1024]{2,1,0:T(8,128)(2,1)} %slice.34) | data formatting | bytes 8388608
  171.3 7.4 %convert_bitcast_fusion = bf16[1024,2048]{1,0:T(8,128)(2,1)S(1)} fusion(bf16[1024,2048]{0,1:T(8,128)(2,1)} %bitcast.62, bf16[2,1024,1024]{2,1,0:T(8,128)(2,1)} %all-gather.5.cloned.1.call-done), kind=kOutput, calls=%fused_computation.2 | convolution fusion | flops 4297064448 | bytes 10485760 | tf_op jit(solution)/shard_map/dot_general | solution.py:10
  178.7 0.0 copy-start
  178.7 2.0 copy-done
  180.7 1.5 slice.36
  182.2 8.0 %fusion.3 = bf16[1024,1024]{0,1:T(8,128)(2,1)S(1)} fusion(bf16[3,1024,1024]{2,1,0:T(8,128)(2,1)} %all-gather.3.cloned.1.call-done, bf16[2,1024,1024]{2,1,0:T(8,128)(2,1)} %all-gather.5.cloned.1.call-done, bf16[1024,2048]{1,0:T(8,128)(2,1)} %copy-done), kind=kOutput, calls=%fused_computation.7 | convolution fusion | flops 4299161600 | bytes 10485760 | tf_op jit(solution)/shard_map/dot_general | solution.py:10
  190.2 0.8 dynamic-slice_bitcast_fusion.2
  191.0 0.8 dynamic-slice_bitcast_fusion
  191.8 1.0 constant_dynamic-slice_fusion
  192.8 5.5 %collective-permute-start.1 = (bf16[1024,128]{1,0:T(8,128)(2,1)}, bf16[1024,128]{1,0:T(8,128)(2,1)S(1)}, u32[]{:S(2)}, u32[]{:S(2)}) collective-permute-start(bf16[1024,128]{1,0:T(8,128)(2,1)} %dynamic-slice_bitcast_fusion), channel_id=1, source_target_pairs={{0,0},{1,1},{2,2},{3,3},{4,4},{5,5},{6,6},{7,7},{8,64},{9,65},{10,... | collective-permute-start | bytes 786440 | tf_op jit(solution)/shard_map/ppermute | solution.py:42
  198.2 3.2 %collective-permute-start = (bf16[1024,128]{1,0:T(8,128)(2,1)S(1)}, bf16[1024,128]{1,0:T(8,128)(2,1)}, u32[]{:S(2)}, u32[]{:S(2)}) collective-permute-start(bf16[1024,128]{1,0:T(8,128)(2,1)S(1)} %constant_dynamic-slice_fusion), channel_id=1, source_target_pairs={{0,0},{1,1},{2,2},{3,3},{4,4},{5,5},{6,6},{7,7},{8,64},{9,65},{10,... | collective-permute-start | bytes 786440 | tf_op jit(solution)/shard_map/ppermute | solution.py:41
  201.5 0.6 pad_maximum_fusion.2
  202.1 0.0 copy-done.2
  202.1 2.3 convolution_subtract_fusion.1
  204.5 4.5 %fusion.16 = bf16[128,1024]{0,1:T(8,128)(2,1)S(1)} fusion(bf16[2,1024,1024]{2,1,0:T(8,128)(2,1)} %all-gather.5.cloned.1.call-done, bf16[1024,128]{1,0:T(8,128)(2,1)} %copy-done.2, bf16[1024,2048]{1,0:T(8,128)(2,1)} %copy-done, bf16[2,1024,128]{2,1,0:T(8,128)(2,1)} %param.12), kind=kOutput, calls=%fused_computation.19 | convolution fusion | flops 537395200 | bytes 4980736 | tf_op jit(solution)/shard_map/dot_general | solution.py:10
  209.0 1.8 pad_maximum_fusion
  210.8 0.0 copy-start.1
  210.8 0.0 copy-start.3
  210.8 1.5 convolution_subtract_fusion
  212.3 33.1 %collective-permute-done.1 = bf16[1024,128]{1,0:T(8,128)(2,1)S(1)} collective-permute-done((bf16[1024,128]{1,0:T(8,128)(2,1)}, bf16[1024,128]{1,0:T(8,128)(2,1)S(1)}, u32[]{:S(2)}, u32[]{:S(2)}) %collective-permute-start.1) | collective-permute-done | bytes 262176 | tf_op jit(solution)/shard_map/ppermute | solution.py:42
  245.4 0.7 fusion.36
  246.2 4.4 %collective-permute-done = bf16[1024,128]{1,0:T(8,128)(2,1)} collective-permute-done((bf16[1024,128]{1,0:T(8,128)(2,1)S(1)}, bf16[1024,128]{1,0:T(8,128)(2,1)}, u32[]{:S(2)}, u32[]{:S(2)}) %collective-permute-start) | collective-permute-done | bytes 262176 | tf_op jit(solution)/shard_map/ppermute | solution.py:41
  250.6 0.0 copy-done.1
  250.6 0.0 copy-done.3
  250.6 2.5 fusion.15
  (3 shorter events, 0.0 us)
Async XLA Ops:
  7.2 65.7 %all-gather.5.cloned.1.call-start = ((), (), s32[]{:S(2)}) async-start(), calls=%async_computation.2 | async-start | bytes 4718592 | tf_op jit(solution)/shard_map/all_gather | solution.py:29
  7.9 152.5 %all-gather.3.cloned.1.call-start = ((), (), s32[]{:S(2)}) async-start(), calls=%async_computation.1 | async-start | bytes 6389760 | tf_op jit(solution)/shard_map/all_gather | solution.py:32
  75.2 127.0 %copy-start.2 = (bf16[1024,128]{1,0:T(8,128)(2,1)}, bf16[1024,128]{1,0:T(8,128)(2,1)S(1)}, u32[]{:S(2)}) copy-start(bf16[1024,128]{1,0:T(8,128)(2,1)S(1)} %fusion.17) | copy-start | bytes 786436
  178.7 2.1 copy-start
  192.8 52.7 %collective-permute-start.1 = (bf16[1024,128]{1,0:T(8,128)(2,1)}, bf16[1024,128]{1,0:T(8,128)(2,1)S(1)}, u32[]{:S(2)}, u32[]{:S(2)}) collective-permute-start(bf16[1024,128]{1,0:T(8,128)(2,1)} %dynamic-slice_bitcast_fusion), channel_id=1, source_target_pairs={{0,0},{1,1},{2,2},{3,3},{4,4},{5,5},{6,6},{7,7},{8,64},{9,65},{10,... | collective-permute-start | bytes 786440 | tf_op jit(solution)/shard_map/ppermute | solution.py:42
  198.2 52.3 %collective-permute-start = (bf16[1024,128]{1,0:T(8,128)(2,1)S(1)}, bf16[1024,128]{1,0:T(8,128)(2,1)}, u32[]{:S(2)}, u32[]{:S(2)}) collective-permute-start(bf16[1024,128]{1,0:T(8,128)(2,1)S(1)} %constant_dynamic-slice_fusion), channel_id=1, source_target_pairs={{0,0},{1,1},{2,2},{3,3},{4,4},{5,5},{6,6},{7,7},{8,64},{9,65},{10,... | collective-permute-start | bytes 786440 | tf_op jit(solution)/shard_map/ppermute | solution.py:41
  210.8 39.7 %copy-start.1 = (bf16[1024,2048]{1,0:T(8,128)(2,1)S(1)}, bf16[1024,2048]{1,0:T(8,128)(2,1)}, u32[]{:S(2)}) copy-start(bf16[1024,2048]{1,0:T(8,128)(2,1)} %copy-done) | copy-start | bytes 12582916
  210.8 39.7 %copy-start.3 = (bf16[1024,128]{1,0:T(8,128)(2,1)S(1)}, bf16[1024,128]{1,0:T(8,128)(2,1)}, u32[]{:S(2)}) copy-start(bf16[1024,128]{1,0:T(8,128)(2,1)} %param.10) | copy-start | bytes 786436
Sparse Core Ops, SparseCore 0:
  10.1 62.7 all-gather.4
  76.8 83.5 all-gather.2
where the time goes:
time: 261 us; the launch traced here: 260 us
  waiting for transfers between devices  168 us (64%)
  matrix products  29.4 us (11%)
  blocking collectives  18.1 us (7%)
  local copies, waits for them, and re-layouts  17.6 us (7%)
  between operations  14.1 us (5%)
  starting transfers between devices  8.8 us (3%)
  other arithmetic  3.86 us (1%)
    all_gather x1, waiting for transfers between devices, per_device(): panels = lax.all_gather(panels, ('y', 'core', 'vox'), axis=1, tiled=True)  85.2 us
    all_gather x1, waiting for transfers between devices, per_device(): whole = lax.all_gather(inverses, 'row', axis=1, tiled=True)  44.6 us
    ppermute x1, waiting for transfers between devices, per_device(): lax.ppermute(lax.dynamic_slice_in_dim(second_low, start, rest_cols, 1), a...  33.1 us
    dot_general x8, matrix products, contract(): lax.dot_general(left, right, (dims, ((), ())), preferred_element_type=jnp...  29.4 us
    all_to_all x1, blocking collectives, gather_small(): out = lax.all_to_all(jnp.tile(block, (size, 1)), axis, 0, 0, tiled=True)  18.1 us
    unnamed x9, local copies, waits for them, and re-layouts  8.24 us
    ppermute x1, starting transfers between devices, per_device(): lax.ppermute(lax.dynamic_slice_in_dim(second_low, start, rest_cols, 1), a...  5.48 us
  transfers between devices with their start and end apart: 4, of which 4 were waited for; matrix products, arithmetic and copies ran while one was open for 6% of the time, Pallas kernels for 0%

commit v1 on v0

--- a/solution.py
+++ b/solution.py
@@ -4,6 +4,17 @@
 from jax import lax
 from jax.sharding import Mesh
 from jax.sharding import PartitionSpec as P
+
+
+def pass_along(x, name, along):
+    n_dev = lax.axis_size(name)
+    right = [(i, (i + 1) % n_dev) for i in range(n_dev)]
+    parts = [x]
+    for hop in range(1, n_dev):
+        parts = [lax.ppermute(parts[0], name, right), *parts]
+    result = jnp.concatenate(parts, axis=along)
+    shift = (lax.axis_index(name) + 1) * parts[-1].shape[along]
+    return jnp.roll(result, shift, axis=along)
 
 
 def contract(left, right, dims):
@@ -26,7 +37,7 @@
     width = panel_low.shape[1]
     rest_cols = gram_rest.shape[1]
     bf16 = jnp.bfloat16
-    whole = lax.all_gather(inverses, "row", axis=1, tiled=True)
+    whole = pass_along(inverses, "row", 1)
     top = gather_small(panel_top.T, "row", rows).transpose(1, 0, 2).reshape(width, -1)
     panels = jnp.stack([top, panel_low.T, panel_next.T])
     panels = lax.all_gather(panels, ("y", "core", "vox"), axis=1, tiled=True)

time: 261 us -> 223 us (0.85)
  the two profiles are of different devices: /device:TPU:16 before, /device:TPU:23 now
where the time goes in v1:
time: 223 us
  waiting for transfers between devices  118 us (53%)
  matrix products  25.2 us (11%)
  local copies, waits for them, and re-layouts  24 us (11%)
  starting transfers between devices  21.9 us (10%)
  blocking collectives  16.7 us (7%)
  between operations  14.4 us (6%)
  other arithmetic  2.91 us (1%)
    ppermute x7, waiting for transfers between devices, pass_along(): parts = [lax.ppermute(parts[0], name, right), *parts]  74.7 us
    ppermute x1, waiting for transfers between devices, per_device(): lax.ppermute(lax.dynamic_slice_in_dim(second_low, start, rest_cols, 1), a...  37.9 us
    dot_general x8, matrix products, contract(): lax.dot_general(left, right, (dims, ((), ())), preferred_element_type=jnp...  25.2 us
    all_to_all x1, blocking collectives, gather_small(): out = lax.all_to_all(jnp.tile(block, (size, 1)), axis, 0, 0, tiled=True)  16.7 us
    unnamed x32, local copies, waits for them, and re-layouts  15.2 us
    ppermute x7, starting transfers between devices, pass_along(): parts = [lax.ppermute(parts[0], name, right), *parts]  13.6 us
    ppermute x1, starting transfers between devices, per_device(): lax.ppermute(lax.dynamic_slice_in_dim(first_low, start, rest_cols, 1), ax...  6.06 us
    ppermute x1, waiting for transfers between devices, per_device(): lax.ppermute(lax.dynamic_slice_in_dim(first_low, start, rest_cols, 1), ax...  4.88 us
  transfers between devices with their start and end apart: 10, of which 9 were waited for; matrix products, arithmetic and copies ran while one was open for 5% of the time, Pallas kernels for 0%

profile of v1, /device:TPU:23, one launch (start us, length us, event | category | flops | bytes accessed | tf_op | source)
XLA Modules:
  0.0 222.6 jit_solution(862702829850397542)
XLA Ops:
  7.2 0.0 copy-start
  7.2 0.0 all-gather.2.cloned.1.call-start
  7.2 0.7 tile.2
  8.0 16.7 %all_to_all.6 = bf16[8,16,128]{2,1,0:T(8,128)(2,1)S(1)} all-to-all(bf16[8,16,128]{2,1,0:T(8,128)(2,1)S(1)} %tile.2), channel_id=1, replica_groups=mesh['row'=8,'y'=8,'core'=2,'vox'=4] {'row'}, dimensions={0} | all-to-all | bytes 65536 | tf_op jit(solution)/shard_map/all_to_all | solution.py:25
  24.7 1.4 pad_maximum_fusion.1
  26.1 0.0 all-gather.2.cloned.1.call-update
  26.2 2.2 collective-permute-start
  28.4 12.4 %collective-permute-done = bf16[2,128,1024]{2,1,0:T(8,128)(2,1)S(1)} collective-permute-done((bf16[2,128,1024]{2,1,0:T(8,128)(2,1)}, bf16[2,128,1024]{2,1,0:T(8,128)(2,1)S(1)}, u32[]{:S(2)}, u32[]{:S(2)}) %collective-permute-start) | collective-permute-done | bytes 524320 | tf_op jit(solution)/shard_map/ppermute | solution.py:14
  40.8 1.9 collective-permute-start.1
  42.7 11.7 %collective-permute-done.1 = bf16[2,128,1024]{2,1,0:T(8,128)(2,1)S(1)} collective-permute-done((bf16[2,128,1024]{2,1,0:T(8,128)(2,1)S(1)}, bf16[2,128,1024]{2,1,0:T(8,128)(2,1)S(1)}, u32[]{:S(2)}, u32[]{:S(2)}) %collective-permute-start.1) | collective-permute-done | bytes 524320 | tf_op jit(solution)/shard_map/ppermute | solution.py:14
  54.4 1.9 collective-permute-start.2
  56.3 10.7 %collective-permute-done.2 = bf16[2,128,1024]{2,1,0:T(8,128)(2,1)S(1)} collective-permute-done((bf16[2,128,1024]{2,1,0:T(8,128)(2,1)S(1)}, bf16[2,128,1024]{2,1,0:T(8,128)(2,1)S(1)}, u32[]{:S(2)}, u32[]{:S(2)}) %collective-permute-start.2) | collective-permute-done | bytes 524320 | tf_op jit(solution)/shard_map/ppermute | solution.py:14
  67.0 1.9 collective-permute-start.3
  69.0 9.8 %collective-permute-done.3 = bf16[2,128,1024]{2,1,0:T(8,128)(2,1)S(1)} collective-permute-done((bf16[2,128,1024]{2,1,0:T(8,128)(2,1)S(1)}, bf16[2,128,1024]{2,1,0:T(8,128)(2,1)S(1)}, u32[]{:S(2)}, u32[]{:S(2)}) %collective-permute-start.3) | collective-permute-done | bytes 524320 | tf_op jit(solution)/shard_map/ppermute | solution.py:14
  78.8 1.9 collective-permute-start.4
  80.7 9.2 %collective-permute-done.4 = bf16[2,128,1024]{2,1,0:T(8,128)(2,1)S(1)} collective-permute-done((bf16[2,128,1024]{2,1,0:T(8,128)(2,1)S(1)}, bf16[2,128,1024]{2,1,0:T(8,128)(2,1)S(1)}, u32[]{:S(2)}, u32[]{:S(2)}) %collective-permute-start.4) | collective-permute-done | bytes 524320 | tf_op jit(solution)/shard_map/ppermute | solution.py:14
  89.9 1.9 collective-permute-start.5
  91.8 10.0 %collective-permute-done.5 = bf16[2,128,1024]{2,1,0:T(8,128)(2,1)} collective-permute-done((bf16[2,128,1024]{2,1,0:T(8,128)(2,1)S(1)}, bf16[2,128,1024]{2,1,0:T(8,128)(2,1)}, u32[]{:S(2)}, u32[]{:S(2)}) %collective-permute-start.5) | collective-permute-done | bytes 524320 | tf_op jit(solution)/shard_map/ppermute | solution.py:14
  101.8 1.9 collective-permute-start.6
  103.7 10.9 %collective-permute-done.6 = bf16[2,128,1024]{2,1,0:T(8,128)(2,1)} collective-permute-done((bf16[2,128,1024]{2,1,0:T(8,128)(2,1)}, bf16[2,128,1024]{2,1,0:T(8,128)(2,1)}, u32[]{:S(2)}, u32[]{:S(2)}) %collective-permute-start.6) | collective-permute-done | bytes 524320 | tf_op jit(solution)/shard_map/ppermute | solution.py:14
  114.6 1.1 constant_dynamic-update-slice_fusion.15
  115.7 1.1 constant_dynamic-update-slice_fusion.14
  116.9 0.0 copy-start.4
  117.1 1.1 constant_dynamic-update-slice_fusion.7
  118.1 1.1 constant_dynamic-update-slice_fusion.6
  119.5 3.2 %copy-done.3 = bf16[2,2048,1024]{2,1,0:T(8,128)(2,1)} copy-done((bf16[2,2048,1024]{2,1,0:T(8,128)(2,1)}, bf16[2,2048,1024]{2,1,0:T(8,128)(2,1)S(1)}, u32[]{:S(2)}) %copy-start.3) | copy-done | bytes 8388632
  122.7 0.7 fusion.17
  123.4 0.0 all-gather.2.cloned.1.call-done
  123.5 4.6 %slice.34 = bf16[2,1024,1024]{2,1,0:T(8,128)(2,1)} slice(bf16[3,1024,1024]{2,1,0:T(8,128)(2,1)} %all-gather.2.cloned.1.call-done), slice={[0:2], [0:1024], [0:1024]} | slice | bytes 8388608 | tf_op jit(solution)/shard_map/slice | solution.py:44
  128.1 6.2 %copy.17 = bf16[2,1024,1024]{1,2,0:T(8,128)(2,1)} copy(bf16[2,1024,1024]{2,1,0:T(8,128)(2,1)} %slice.34) | data formatting | bytes 8388608
  134.3 7.4 %convolution_convert_fusion = bf16[1024,2048]{1,0:T(8,128)(2,1)S(1)} fusion(bf16[1024,2048]{0,1:T(8,128)(2,1)} %bitcast.58, bf16[2,2048,1024]{2,1,0:T(8,128)(2,1)} %copy-done.3, s32[]{:T(128)S(6)} %select_n.22), kind=kOutput, calls=%fused_computation.2 | convolution fusion | flops 4297064448 | bytes 10485764 | tf_op jit(solution)/shard_map/dot_general | solution.py:21
  141.7 1.6 slice.35
  143.3 1.0 copy-done.1
  144.3 0.7 convolution_subtract_fusion.1
  145.0 4.5 %fusion.16 = bf16[1024,128]{1,0:T(8,128)(2,1)S(1)} fusion(bf16[2,2048,1024]{2,1,0:T(8,128)(2,1)} %copy-done.3, s32[]{:T(128)S(6)} %add.38, s32[]{:T(128)S(6)} %select_n.22, bf16[1024,128]{1,0:T(8,128)(2,1)S(1)} %fusion.17, bf16[1024,2048]{1,0:T(8,128)(2,1)} %copy-done.1, bf16[2,1024,128]{2,1,0:T(8,128)(2,1)S(1)} %copy-done.5), kind=kOutput, calls=%fused_computation.19 | convolution fusion | flops 537395200 | bytes 4980744 | tf_op jit(solution)/shard_map/dot_general | solution.py:21
  149.5 8.0 %fusion.3 = bf16[1024,1024]{1,0:T(8,128)(2,1)S(1)} fusion(bf16[3,1024,1024]{2,1,0:T(8,128)(2,1)} %all-gather.2.cloned.1.call-done, bf16[2,2048,1024]{2,1,0:T(8,128)(2,1)} %copy-done.3, s32[]{:T(128)S(6)} %add.38, s32[]{:T(128)S(6)} %select_n.22, bf16[1024,2048]{1,0:T(8,128)(2,1)} %copy-done.1), kind=kOutput, calls=%fused_computation.7 | convolution fusion | flops 4299161600 | bytes 10485768 | tf_op jit(solution)/shard_map/dot_general | solution.py:21
  157.6 0.1 constant_dynamic-slice_fusion
  157.7 2.2 collective-permute-start.8
  159.9 1.0 constant_dynamic-slice_fusion.1
  160.9 6.1 %collective-permute-start.7 = (bf16[1024,128]{1,0:T(8,128)(2,1)S(1)}, bf16[1024,128]{1,0:T(8,128)(2,1)S(1)}, u32[]{:S(2)}, u32[]{:S(2)}) collective-permute-start(bf16[1024,128]{1,0:T(8,128)(2,1)S(1)} %constant_dynamic-slice_fusion.1), channel_id=1, source_target_pairs={{0,0},{1,1},{2,2},{3,3},{4,4},{5,5},{6,6},{7,7},{8,64},{9,65},{10,... | collective-permute-start | bytes 786440 | tf_op jit(solution)/shard_map/ppermute | solution.py:52
  166.9 0.8 dynamic-slice_bitcast_fusion.10
  167.7 0.8 pad_maximum_fusion
  168.5 0.6 pad_maximum_fusion.2
  169.2 1.5 convolution_subtract_fusion
  170.7 37.9 %collective-permute-done.8 = bf16[1024,128]{1,0:T(8,128)(2,1)S(1)} collective-permute-done((bf16[1024,128]{1,0:T(8,128)(2,1)S(1)}, bf16[1024,128]{1,0:T(8,128)(2,1)S(1)}, u32[]{:S(2)}, u32[]{:S(2)}) %collective-permute-start.8) | collective-permute-done | bytes 262176 | tf_op jit(solution)/shard_map/ppermute | solution.py:53
  208.6 0.7 fusion.40
  209.3 4.9 %collective-permute-done.7 = bf16[1024,128]{1,0:T(8,128)(2,1)S(1)} collective-permute-done((bf16[1024,128]{1,0:T(8,128)(2,1)S(1)}, bf16[1024,128]{1,0:T(8,128)(2,1)S(1)}, u32[]{:S(2)}, u32[]{:S(2)}) %collective-permute-start.7) | collective-permute-done | bytes 262176 | tf_op jit(solution)/shard_map/ppermute | solution.py:52
  214.2 1.5 fusion.15
  (26 shorter events, 0.5 us)
Async XLA Ops:
  7.2 109.9 %copy-start = (bf16[2,128,1024]{2,1,0:T(8,128)(2,1)S(1)}, bf16[2,128,1024]{2,1,0:T(8,128)(2,1)}, u32[]{:S(2)}) copy-start(bf16[2,128,1024]{2,1,0:T(8,128)(2,1)} %param.11) | copy-start | bytes 1572868
  7.2 116.3 %all-gather.2.cloned.1.call-start = ((), (), s32[]{:S(2)}) async-start(), calls=%async_computation.1 | async-start | bytes 6389760 | tf_op jit(solution)/shard_map/all_gather | solution.py:43
  26.2 14.6 %collective-permute-start = (bf16[2,128,1024]{2,1,0:T(8,128)(2,1)}, bf16[2,128,1024]{2,1,0:T(8,128)(2,1)S(1)}, u32[]{:S(2)}, u32[]{:S(2)}) collective-permute-start(bf16[2,128,1024]{2,1,0:T(8,128)(2,1)} %param.11), channel_id=1, source_target_pairs={{0,64},{64,128},{128,192},{192,256},{256,320},{320,384},{384,448},... | collective-permute-start | bytes 1572872 | tf_op jit(solution)/shard_map/ppermute | solution.py:14
  40.8 13.6 %collective-permute-start.1 = (bf16[2,128,1024]{2,1,0:T(8,128)(2,1)S(1)}, bf16[2,128,1024]{2,1,0:T(8,128)(2,1)S(1)}, u32[]{:S(2)}, u32[]{:S(2)}) collective-permute-start(bf16[2,128,1024]{2,1,0:T(8,128)(2,1)S(1)} %collective-permute-done), channel_id=1, source_target_pairs={{0,64},{64,128},{128,192},{192,256},{256,320},{320,384},{384,448},... | collective-permute-start | bytes 1572872 | tf_op jit(solution)/shard_map/ppermute | solution.py:14
  54.4 12.7 %collective-permute-start.2 = (bf16[2,128,1024]{2,1,0:T(8,128)(2,1)S(1)}, bf16[2,128,1024]{2,1,0:T(8,128)(2,1)S(1)}, u32[]{:S(2)}, u32[]{:S(2)}) collective-permute-start(bf16[2,128,1024]{2,1,0:T(8,128)(2,1)S(1)} %collective-permute-done.1), channel_id=1, source_target_pairs={{0,64},{64,128},{128,192},{192,256},{256,320},{320,384},{384,448},... | collective-permute-start | bytes 1572872 | tf_op jit(solution)/shard_map/ppermute | solution.py:14
  67.0 11.7 %collective-permute-start.3 = (bf16[2,128,1024]{2,1,0:T(8,128)(2,1)S(1)}, bf16[2,128,1024]{2,1,0:T(8,128)(2,1)S(1)}, u32[]{:S(2)}, u32[]{:S(2)}) collective-permute-start(bf16[2,128,1024]{2,1,0:T(8,128)(2,1)S(1)} %collective-permute-done.2), channel_id=1, source_target_pairs={{0,64},{64,128},{128,192},{192,256},{256,320},{320,384},{384,448},... | collective-permute-start | bytes 1572872 | tf_op jit(solution)/shard_map/ppermute | solution.py:14
  78.8 11.1 %collective-permute-start.4 = (bf16[2,128,1024]{2,1,0:T(8,128)(2,1)S(1)}, bf16[2,128,1024]{2,1,0:T(8,128)(2,1)S(1)}, u32[]{:S(2)}, u32[]{:S(2)}) collective-permute-start(bf16[2,128,1024]{2,1,0:T(8,128)(2,1)S(1)} %collective-permute-done.3), channel_id=1, source_target_pairs={{0,64},{64,128},{128,192},{192,256},{256,320},{320,384},{384,448},... | collective-permute-start | bytes 1572872 | tf_op jit(solution)/shard_map/ppermute | solution.py:14
  89.9 11.9 %collective-permute-start.5 = (bf16[2,128,1024]{2,1,0:T(8,128)(2,1)S(1)}, bf16[2,128,1024]{2,1,0:T(8,128)(2,1)}, u32[]{:S(2)}, u32[]{:S(2)}) collective-permute-start(bf16[2,128,1024]{2,1,0:T(8,128)(2,1)S(1)} %collective-permute-done.4), channel_id=1, source_target_pairs={{0,64},{64,128},{128,192},{192,256},{256,320},{320,384},{384,448},... | collective-permute-start | bytes 1572872 | tf_op jit(solution)/shard_map/ppermute | solution.py:14
  101.8 12.8 %collective-permute-start.6 = (bf16[2,128,1024]{2,1,0:T(8,128)(2,1)}, bf16[2,128,1024]{2,1,0:T(8,128)(2,1)}, u32[]{:S(2)}, u32[]{:S(2)}) collective-permute-start(bf16[2,128,1024]{2,1,0:T(8,128)(2,1)} %collective-permute-done.5), channel_id=1, source_target_pairs={{0,64},{64,128},{128,192},{192,256},{256,320},{320,384},{384,448},... | collective-permute-start | bytes 1572872 | tf_op jit(solution)/shard_map/ppermute | solution.py:14
  116.9 5.9 %copy-start.4 = (bf16[2,1024,128]{2,1,0:T(8,128)(2,1)S(1)}, bf16[2,1024,128]{2,1,0:T(8,128)(2,1)}, u32[]{:S(2)}) copy-start(bf16[2,1024,128]{2,1,0:T(8,128)(2,1)} %param.12) | copy-start | bytes 1572868
  119.5 3.2 %copy-start.3 = (bf16[2,2048,1024]{2,1,0:T(8,128)(2,1)}, bf16[2,2048,1024]{2,1,0:T(8,128)(2,1)S(1)}, u32[]{:S(2)}) copy-start(bf16[2,2048,1024]{2,1,0:T(8,128)(2,1)S(1)} %constant_dynamic-update-slice_fusion) | copy-start | bytes 25165828
  134.3 10.0 %copy-start.6 = (bf16[1024,128]{1,0:T(8,128)(2,1)S(1)}, bf16[1024,128]{1,0:T(8,128)(2,1)}, u32[]{:S(2)}) copy-start(bf16[1024,128]{1,0:T(8,128)(2,1)} %param.13) | copy-start | bytes 786436
  141.7 2.6 %copy-start.1 = (bf16[1024,2048]{1,0:T(8,128)(2,1)}, bf16[1024,2048]{1,0:T(8,128)(2,1)S(1)}, u32[]{:S(2)}) copy-start(bf16[1024,2048]{1,0:T(8,128)(2,1)S(1)} %convolution_convert_fusion) | copy-start | bytes 12582916
  141.7 3.3 %copy-start.5 = (bf16[2,1024,128]{2,1,0:T(8,128)(2,1)S(1)}, bf16[2,1024,128]{2,1,0:T(8,128)(2,1)}, u32[]{:S(2)}) copy-start(bf16[2,1024,128]{2,1,0:T(8,128)(2,1)} %param.12) | copy-start | bytes 1572868
  157.7 56.5 %copy-start.2 = (bf16[1024,2048]{1,0:T(8,128)(2,1)S(1)}, bf16[1024,2048]{1,0:T(8,128)(2,1)}, u32[]{:S(2)}) copy-start(bf16[1024,2048]{1,0:T(8,128)(2,1)} %copy-done.1) | copy-start | bytes 12582916
  157.7 56.5 %copy-start.7 = (bf16[1024,128]{1,0:T(8,128)(2,1)S(1)}, bf16[1024,128]{1,0:T(8,128)(2,1)}, u32[]{:S(2)}) copy-start(bf16[1024,128]{1,0:T(8,128)(2,1)} %param.10) | copy-start | bytes 786436
  157.7 50.9 %collective-permute-start.8 = (bf16[1024,128]{1,0:T(8,128)(2,1)S(1)}, bf16[1024,128]{1,0:T(8,128)(2,1)S(1)}, u32[]{:S(2)}, u32[]{:S(2)}) collective-permute-start(bf16[1024,128]{1,0:T(8,128)(2,1)S(1)} %constant_dynamic-slice_fusion), channel_id=1, source_target_pairs={{0,0},{1,1},{2,2},{3,3},{4,4},{5,5},{6,6},{7,7},{8,64},{9,65},{10,... | collective-permute-start | bytes 786440 | tf_op jit(solution)/shard_map/ppermute | solution.py:53
  160.9 53.3 %collective-permute-start.7 = (bf16[1024,128]{1,0:T(8,128)(2,1)S(1)}, bf16[1024,128]{1,0:T(8,128)(2,1)S(1)}, u32[]{:S(2)}, u32[]{:S(2)}) collective-permute-start(bf16[1024,128]{1,0:T(8,128)(2,1)S(1)} %constant_dynamic-slice_fusion.1), channel_id=1, source_target_pairs={{0,0},{1,1},{2,2},{3,3},{4,4},{5,5},{6,6},{7,7},{8,64},{9,65},{10,... | collective-permute-start | bytes 786440 | tf_op jit(solution)/shard_map/ppermute | solution.py:52
Sparse Core Ops, SparseCore 0:
  26.3 81.5 all-gather.1
